TPU v7x, 32 devices: a whole 2x2x4 slice. The times are simulated.
32 devices in a mesh: near: 16 (over z, y, x), far: 2 (over core).
Axes of the slice: x: 2, y: 2, z: 4, core: 2. Of those that a mesh axis runs over, the one named last changes fastest.
Arguments:
- vectors: bfloat16 [128, 4, 480], P('near'), may hold values from -6 to 6
- near_blocks: bfloat16 [128, 16, 2, 240, 240], P('near', 'far'), may hold values from -0.09375 to 0.09375
- neighbours: int32 [128, 16], P('near', 'far'), may hold values from 0 to 127, as said below
- live_counts: int32 [128], P('near'), may hold values from 4 to 16, as said below
- tmatrix: float32 [128, 2, 240], P('near'), may hold values from -0.8 to 0.8
- agg_matrix: bfloat16 [480, 512], replicated, may hold values from -0.25 to 0.25
- sphere_box: int32 [128], P('near'), may hold values from 0 to 15, never falling along the last dimension, each value on 1 to 24 neighbouring positions
- agg_angle: float32 [128, 256], P('near'), may hold values from -3.140625 to 3.140625
- far_list: int32 [16, 16], P('far'), may hold values from 0 to 15, as said below
- far_factors: float32 [16, 16, 2, 256], P('far', None, None, 'near'), may hold values from -0.6 to 0.6
- dis_matrix: bfloat16 [512, 480], replicated, may hold values from -0.25 to 0.25
Outputs:
- first_image: bfloat16 [128, 4, 480], P('near')
- second_image: bfloat16 [128, 4, 480], P('near')
Inputs may be any that keep to these rules, and one draw needn't show every extreme that they name: `neighbours`: each entry differs from its row's sphere number by 1 to 8. `live_counts`: slots at or above a sphere's count are padding; some sphere has all 16 slots live. `sphere_box`: box numbers never fall along the spheres; every box holds 1 to 24 spheres. `far_list`: a box's far list names neither the box nor the boxes numbered one above or below it, counted around.
All inputs are finite; a program needn't handle non-finite values.
Results may differ from a plain program's by a relative error of at most 0.0052.
Values may be sent and summed in bfloat16 or wider, within the bound.
No kernel may reach another device: no remote copies, remote signals or barrier semaphores. Data moves between devices by JAX's collectives and lax.ppermute only.
A program may use at most 64 MiB of HBM per device.

v0:
```python
import jax
import jax.numpy as jnp
from jax import lax
from jax.sharding import PartitionSpec as P


def with_halo(block, sides, width):
    for axis, dim in sides:
        count = lax.axis_size(axis)
        forward = [(i, i + 1) for i in range(count - 1)]
        backward = [(target, source) for source, target in forward]
        low = lax.ppermute(
            lax.slice_in_dim(block, block.shape[dim] - width, None, axis=dim), axis, forward
        )
        high = lax.ppermute(lax.slice_in_dim(block, 0, width, axis=dim), axis, backward)
        block = jnp.concatenate([low, block, high], axis=dim)
    return block


def complex_mul(left_re, left_im, right_re, right_im):
    return (left_re * right_re - left_im * right_im, left_re * right_im + left_im * right_re)


def outgoing_of(rows_vec, cos_rows, sin_rows, agg_matrix):
    count, newton, width = rows_vec.shape
    waves = agg_matrix.shape[1] // 2
    product = jnp.dot(
        rows_vec.reshape(count * newton, width), agg_matrix, preferred_element_type=jnp.float32
    )
    product = product.reshape(count, newton, 2, waves)
    out_re, out_im = complex_mul(
        product[:, :, 0], product[:, :, 1], cos_rows[:, None, :], sin_rows[:, None, :]
    )
    return jnp.stack([out_re, out_im], axis=2)


def apply_operator(
    current,
    near_blocks,
    neighbours,
    live_counts,
    tmatrix,
    agg_matrix,
    sphere_box,
    agg_angle,
    far_list,
    far_factors,
    dis_matrix,
):
    sph_count, newton, width = current.shape
    coeffs = width // 2
    slots = neighbours.shape[1]
    own_boxes = far_list.shape[0]
    far_count = lax.axis_size("far")
    all_boxes = own_boxes * far_count
    waves = agg_matrix.shape[1] // 2
    near_pos = lax.axis_index("near")
    far_pos = lax.axis_index("far")
    padded = with_halo(current, (("near", 0),), sph_count)
    local_index = neighbours - (near_pos - 1) * sph_count
    gathered = padded[local_index]
    alive = (far_pos * slots + jnp.arange(slots, dtype=jnp.int32))[None, :] < live_counts[:, None]
    gathered = jnp.where(alive[:, :, None, None], gathered, jnp.zeros_like(gathered))
    both_parts = jnp.concatenate([gathered[..., :coeffs], gathered[..., coeffs:]], axis=2)
    with_real = jnp.einsum(
        "nkrc,nkcd->nrd", both_parts, near_blocks[:, :, 0], preferred_element_type=jnp.float32
    )
    with_imag = jnp.einsum(
        "nkrc,nkcd->nrd", both_parts, near_blocks[:, :, 1], preferred_element_type=jnp.float32
    )
    near_re = with_real[:, :newton] - with_imag[:, newton:]
    near_im = with_imag[:, :newton] + with_real[:, newton:]
    near_field = jnp.concatenate([near_re, near_im], axis=-1)
    cosine = jnp.cos(agg_angle)
    sine = jnp.sin(agg_angle)
    stacked = outgoing_of(current, cosine, sine, agg_matrix)
    member = (
        sphere_box[None, :] == far_pos * own_boxes + jnp.arange(own_boxes, dtype=jnp.int32)[:, None]
    ).astype(jnp.float32)
    partial_value = jnp.einsum("bn,nrtq->brtq", member, stacked, precision=lax.Precision.HIGHEST)
    box_waves = lax.psum_scatter(partial_value, "near", scatter_dimension=3, tiled=True)
    all_waves = lax.all_gather(box_waves, "far", axis=0, tiled=True)
    selector = (
        far_list[:, :, None] == jnp.arange(all_boxes, dtype=jnp.int32)[None, None, :]
    ).astype(jnp.float32)
    picked = jnp.einsum("gfb,brtq->gfrtq", selector, all_waves, precision=lax.Precision.HIGHEST)
    in_re, in_im = complex_mul(
        far_factors[:, :, None, 0, :],
        far_factors[:, :, None, 1, :],
        picked[:, :, :, 0],
        picked[:, :, :, 1],
    )
    incoming = jnp.stack([jnp.sum(in_re, axis=1), jnp.sum(in_im, axis=1)], axis=2)
    full_waves = lax.all_gather(incoming, "near", axis=3, tiled=True)
    owner = (
        sphere_box[:, None] == far_pos * own_boxes + jnp.arange(own_boxes, dtype=jnp.int32)[None, :]
    ).astype(jnp.float32)
    sphere_waves = jnp.einsum("nb,brtq->nrtq", owner, full_waves, precision=lax.Precision.HIGHEST)
    local_re, local_im = complex_mul(
        sphere_waves[:, :, 0], sphere_waves[:, :, 1], cosine[:, None, :], -sine[:, None, :]
    )
    local_waves = jnp.concatenate([local_re, local_im], axis=-1).astype(jnp.bfloat16)
    far_field = jnp.dot(
        local_waves.reshape(sph_count * newton, 2 * waves),
        dis_matrix,
        preferred_element_type=jnp.float32,
    )
    far_field = far_field.reshape(sph_count, newton, width)
    field = lax.psum(near_field + far_field, "far")
    scat_re, scat_im = complex_mul(
        tmatrix[:, None, 0, :], tmatrix[:, None, 1, :], field[..., :coeffs], field[..., coeffs:]
    )
    image = current.astype(jnp.float32) - jnp.concatenate([scat_re, scat_im], axis=-1)
    return image.astype(jnp.bfloat16)


def shards(
    vectors,
    near_blocks,
    neighbours,
    live_counts,
    tmatrix,
    agg_matrix,
    sphere_box,
    agg_angle,
    far_list,
    far_factors,
    dis_matrix,
):
    first_image = apply_operator(
        vectors,
        near_blocks,
        neighbours,
        live_counts,
        tmatrix,
        agg_matrix,
        sphere_box,
        agg_angle,
        far_list,
        far_factors,
        dis_matrix,
    )
    second_image = apply_operator(
        first_image,
        near_blocks,
        neighbours,
        live_counts,
        tmatrix,
        agg_matrix,
        sphere_box,
        agg_angle,
        far_list,
        far_factors,
        dis_matrix,
    )
    return (first_image, second_image)


def solution(mesh):
    return jax.shard_map(
        shards,
        mesh=mesh,
        in_specs=(
            P("near", None, None),
            P("near", "far", None, None, None),
            P("near", "far"),
            P("near"),
            P("near", None, None),
            P(),
            P("near"),
            P("near", None),
            P("far", None),
            P("far", None, None, "near"),
            P(),
        ),
        out_specs=(P("near", None, None), P("near", None, None)),
        check_vma=False,
    )
```

profile of v0, /device:TPU:0, one launch (start us, length us, event | category | flops | bytes accessed | tf_op | source)
XLA Modules:
  0.0 290.1 jit_solution(10729382742883723635)
XLA Ops:
  7.2 0.0 copy-start
  7.2 0.0 copy-start.1
  7.2 0.0 reduce-scatter.7.cloned.1.call-start
  7.3 5.0 %collective-permute-start = (bf16[8,4,480]{2,1,0:T(4,128)(2,1)}, bf16[8,4,480]{2,1,0:T(4,128)(2,1)S(1)}, u32[]{:S(2)}, u32[]{:S(2)}) collective-permute-start(bf16[8,4,480]{2,1,0:T(4,128)(2,1)} %param.11), channel_id=1, source_target_pairs={{0,2},{2,4},{4,6},{6,8},{8,10},{10,12},{12,14},{14,16},{16,18},{18... | collective-permute-start | bytes 92168 | tf_op jit(solution)/shard_map/ppermute | solution.py:12
  12.3 1.3 collective-permute-start.1
  13.6 0.7 fusion.80
  14.4 1.2 fusion.29
  15.6 0.9 fusion.34
  16.5 0.7 copy.86
  17.2 1.9 reshape.112
  19.2 0.0 reduce-scatter.7.cloned.1.call-update
  19.2 0.0 reduce-scatter.9.cloned.1.call-start
  19.3 1.1 fusion.78
  20.4 0.7 broadcast_compare_fusion
  21.1 0.7 compare_select_fusion
  21.8 0.1 reshape.80
  21.9 0.8 fusion.79
  22.7 0.8 pad_maximum_fusion.6
  23.6 0.8 gather_fusion
  24.4 0.2 broadcast_select_fusion.1
  24.6 0.1 fusion.77
  24.7 4.4 %fusion.12 = f32[8,8,240]{2,1,0:T(8,128)S(1)} fusion(bf16[8,8,2,240,240]{4,3,2,1,0:T(8,128)(2,1)} %param.12, bf16[8,8,4,240]{3,2,1,0:T(4,128)(2,1)S(1)} %get-tuple-element.9, bf16[8,8,4,240]{3,2,1,0:T(4,128)(2,1)S(1)} %get-tuple-element.8), kind=kOutput, calls=%fused_computation.14 | convolution fusion | flops 59473920 | bytes 8171520 | tf_op jit(solution)/shard_map/nkrc,nkcd->nrd/dot_general | solution.py:65
  29.2 4.4 %fusion.18 = f32[8,8,240]{2,1,0:T(8,128)S(1)} fusion(bf16[8,8,2,240,240]{4,3,2,1,0:T(8,128)(2,1)} %param.12, bf16[8,8,4,240]{3,2,1,0:T(4,128)(2,1)S(1)} %get-tuple-element.9, bf16[8,8,4,240]{3,2,1,0:T(4,128)(2,1)S(1)} %get-tuple-element.8), kind=kOutput, calls=%fused_computation.16 | convolution fusion | flops 59473920 | bytes 8171520 | tf_op jit(solution)/shard_map/nkrc,nkcd->nrd/dot_general | solution.py:68
  33.6 65.1 %reduce-scatter.7.cloned.1.call-done = f32[16,64]{1,0:T(8,128)} async-done(((f32[256,64]{1,0:T(8,128)}), f32[16,64]{1,0:T(8,128)}) %reduce-scatter.7.cloned.1.call-update) | async-done | bytes 4112
  98.7 0.8 reshape.113
  99.6 0.1 copy.87
  99.6 1.8 all_gather.12
  101.5 0.4 fusion.44
  101.9 0.2 subtract_reduce_fusion.1
  102.1 0.1 copy.49
  102.2 41.7 %all_gather.13 = f32[8,4,2,256]{0,1,2,3:T(4,128)S(1)} all-gather(f32[8,4,2,16]{0,1,2,3:T(4,128)S(1)} %copy.49), channel_id=1, replica_groups=mesh['near'=16,'far'=2] {'near'}, dimensions={3}, use_global_device_ids=true | all-gather | bytes 69632 | tf_op jit(solution)/shard_map/all_gather | solution.py:94
  143.9 0.7 fusion.26
  144.7 0.3 convolution_add_fusion.1
  144.9 3.6 %psum.14 = f32[8,4,480]{2,1,0:T(4,128)S(1)} all-reduce(f32[8,4,480]{2,1,0:T(4,128)S(1)} %convolution_add_fusion.1), channel_id=1, replica_groups=mesh['near'=16,'far'=2] {'far'}, use_global_device_ids=true, to_apply=%region_3.4 | all-reduce | flops 15360 | bytes 122880 | tf_op jit(solution)/shard_map/psum | solution.py:109
  148.5 0.1 multiply_subtract_fusion.2
  148.6 0.1 fusion.38
  148.7 0.0 copy-start.2
  148.7 4.0 %collective-permute-start.2 = (bf16[8,4,480]{2,1,0:T(4,128)(2,1)S(1)}, bf16[8,4,480]{2,1,0:T(4,128)(2,1)S(1)}, u32[]{:S(2)}, u32[]{:S(2)}) collective-permute-start(bf16[8,4,480]{2,1,0:T(4,128)(2,1)S(1)} %fusion.38), channel_id=1, source_target_pairs={{0,2},{2,4},{4,6},{6,8},{8,10},{10,12},{12,14},{14,16},{16,18},{18... | collective-permute-start | bytes 92168 | tf_op jit(solution)/shard_map/ppermute | solution.py:12
  152.8 1.3 collective-permute-start.3
  154.1 0.2 fusion.28
  154.3 0.2 fusion.39
  154.5 0.7 copy.88
  155.3 1.9 reshape.114
  157.2 0.0 reduce-scatter.9.cloned.1.call-update
  157.3 1.3 collective-permute-done.3
  158.6 0.1 pad_maximum_fusion.7
  158.7 0.8 gather_fusion.1
  159.5 0.2 broadcast_select_fusion
  159.7 0.1 fusion.76
  159.8 4.4 %fusion.15 = f32[8,8,240]{2,1,0:T(8,128)S(1)} fusion(bf16[8,8,2,240,240]{4,3,2,1,0:T(8,128)(2,1)} %param.12, bf16[8,8,4,240]{3,2,1,0:T(4,128)(2,1)S(1)} %get-tuple-element.7, bf16[8,8,4,240]{3,2,1,0:T(4,128)(2,1)S(1)} %get-tuple-element.6), kind=kOutput, calls=%fused_computation.15 | convolution fusion | flops 59473920 | bytes 8171520 | tf_op jit(solution)/shard_map/nkrc,nkcd->nrd/dot_general | solution.py:65
  164.3 4.4 %fusion.21 = f32[8,8,240]{2,1,0:T(8,128)S(1)} fusion(bf16[8,8,2,240,240]{4,3,2,1,0:T(8,128)(2,1)} %param.12, bf16[8,8,4,240]{3,2,1,0:T(4,128)(2,1)S(1)} %get-tuple-element.7, bf16[8,8,4,240]{3,2,1,0:T(4,128)(2,1)S(1)} %get-tuple-element.6), kind=kOutput, calls=%fused_computation.17 | convolution fusion | flops 59473920 | bytes 8171520 | tf_op jit(solution)/shard_map/nkrc,nkcd->nrd/dot_general | solution.py:68
  168.7 64.0 %reduce-scatter.9.cloned.1.call-done = f32[16,64]{1,0:T(8,128)} async-done(((f32[256,64]{1,0:T(8,128)}), f32[16,64]{1,0:T(8,128)}) %reduce-scatter.9.cloned.1.call-update) | async-done | bytes 4112
  232.7 0.8 reshape.115
  233.5 0.1 copy.89
  233.6 1.8 all_gather.14
  235.4 0.4 fusion.46
  235.9 0.2 subtract_reduce_fusion
  236.0 0.1 copy.58
  236.2 41.7 %all_gather.15 = f32[8,4,2,256]{0,1,2,3:T(4,128)S(1)} all-gather(f32[8,4,2,16]{0,1,2,3:T(4,128)S(1)} %copy.58), channel_id=1, replica_groups=mesh['near'=16,'far'=2] {'near'}, dimensions={3}, use_global_device_ids=true | all-gather | bytes 69632 | tf_op jit(solution)/shard_map/all_gather | solution.py:94
  277.9 0.7 fusion.24
  278.6 0.3 convolution_add_fusion
  278.9 3.6 %psum.15 = f32[8,4,480]{2,1,0:T(4,128)S(1)} all-reduce(f32[8,4,480]{2,1,0:T(4,128)S(1)} %convolution_add_fusion), channel_id=1, replica_groups=mesh['near'=16,'far'=2] {'far'}, use_global_device_ids=true, to_apply=%region_7.8 | all-reduce | flops 15360 | bytes 122880 | tf_op jit(solution)/shard_map/psum | solution.py:109
  282.5 0.1 multiply_subtract_fusion
  282.6 0.7 fusion.43
  (26 shorter events, 0.2 us)
Async XLA Ops:
  7.2 137.5 %copy-start = (bf16[512,480]{0,1:T(8,128)(2,1)S(1)}, bf16[512,480]{0,1:T(8,128)(2,1)}, u32[]{:S(2)}) copy-start(bf16[512,480]{0,1:T(8,128)(2,1)} %param.21) | copy-start | bytes 1474564
  7.2 141.4 %copy-start.3 = (bf16[8,4,480]{2,1,0:T(4,128)(2,1)S(1)}, bf16[8,4,480]{2,1,0:T(4,128)(2,1)}, u32[]{:S(2)}) copy-start(bf16[8,4,480]{2,1,0:T(4,128)(2,1)} %param.11) | copy-start | bytes 92164
  7.2 146.9 %copy-start.1 = (bf16[480,512]{1,0:T(8,128)(2,1)S(1)}, bf16[480,512]{1,0:T(8,128)(2,1)}, u32[]{:S(2)}) copy-start(bf16[480,512]{1,0:T(8,128)(2,1)} %param.16) | copy-start | bytes 1474564
  7.2 136.7 %copy-start.5 = (s32[8]{0:T(128)S(1)}, s32[8]{0:T(128)}, u32[]{:S(2)}) copy-start(s32[8]{0:T(128)} %param.17) | copy-start | bytes 100
  7.2 94.3 %copy-start.4 = (s32[8,16]{1,0:T(8,128)S(1)}, s32[8,16]{1,0:T(8,128)}, u32[]{:S(2)}) copy-start(s32[8,16]{1,0:T(8,128)} %param.19) | copy-start | bytes 1540
  7.2 91.5 %reduce-scatter.7.cloned.1.call-start = ((), (), s32[]{:S(2)}) async-start(), calls=%async_computation.2 | async-start | bytes 139264
  7.3 15.5 %collective-permute-start = (bf16[8,4,480]{2,1,0:T(4,128)(2,1)}, bf16[8,4,480]{2,1,0:T(4,128)(2,1)S(1)}, u32[]{:S(2)}, u32[]{:S(2)}) collective-permute-start(bf16[8,4,480]{2,1,0:T(4,128)(2,1)} %param.11), channel_id=1, source_target_pairs={{0,2},{2,4},{4,6},{6,8},{8,10},{10,12},{12,14},{14,16},{16,18},{18... | collective-permute-start | bytes 92168 | tf_op jit(solution)/shard_map/ppermute | solution.py:12
  12.3 10.5 %collective-permute-start.1 = (bf16[8,4,480]{2,1,0:T(4,128)(2,1)}, bf16[8,4,480]{2,1,0:T(4,128)(2,1)S(1)}, u32[]{:S(2)}, u32[]{:S(2)}) collective-permute-start(bf16[8,4,480]{2,1,0:T(4,128)(2,1)} %param.11), channel_id=1, source_target_pairs={{2,0},{4,2},{6,4},{8,6},{10,8},{12,10},{14,12},{16,14},{18,16},{20... | collective-permute-start | bytes 92168 | tf_op jit(solution)/shard_map/ppermute | solution.py:15
  19.2 213.5 %reduce-scatter.9.cloned.1.call-start = ((), (), s32[]{:S(2)}) async-start(), calls=%async_computation.3 | async-start | bytes 139264
  148.7 134.5 %copy-start.2 = (bf16[8,4,480]{2,1,0:T(4,128)(2,1)}, bf16[8,4,480]{2,1,0:T(4,128)(2,1)S(1)}, u32[]{:S(2)}) copy-start(bf16[8,4,480]{2,1,0:T(4,128)(2,1)S(1)} %fusion.38) | copy-start | bytes 92164
  148.7 8.5 %collective-permute-start.2 = (bf16[8,4,480]{2,1,0:T(4,128)(2,1)S(1)}, bf16[8,4,480]{2,1,0:T(4,128)(2,1)S(1)}, u32[]{:S(2)}, u32[]{:S(2)}) collective-permute-start(bf16[8,4,480]{2,1,0:T(4,128)(2,1)S(1)} %fusion.38), channel_id=1, source_target_pairs={{0,2},{2,4},{4,6},{6,8},{8,10},{10,12},{12,14},{14,16},{16,18},{18... | collective-permute-start | bytes 92168 | tf_op jit(solution)/shard_map/ppermute | solution.py:12
  152.8 5.8 %collective-permute-start.3 = (bf16[8,4,480]{2,1,0:T(4,128)(2,1)S(1)}, bf16[8,4,480]{2,1,0:T(4,128)(2,1)S(1)}, u32[]{:S(2)}, u32[]{:S(2)}) collective-permute-start(bf16[8,4,480]{2,1,0:T(4,128)(2,1)S(1)} %fusion.38), channel_id=1, source_target_pairs={{2,0},{4,2},{6,4},{8,6},{10,8},{12,10},{14,12},{16,14},{18,16},{20... | collective-permute-start | bytes 92168 | tf_op jit(solution)/shard_map/ppermute | solution.py:15
Sparse Core Ops, SparseCore 0:
  19.3 79.3 reduce-scatter.6
  157.4 75.2 reduce-scatter.8
where the time goes:
time: 291 us; the launch traced here: 290 us
  waiting for transfers between devices  130 us (45%)
  blocking collectives  94.3 us (32%)
  matrix products  22.9 us (8%)
  between operations  14.5 us (5%)
  local copies, waits for them, and re-layouts  12.1 us (4%)
  starting transfers between devices  11.7 us (4%)
  other arithmetic  4.22 us (1%)
    unnamed x4, waiting for transfers between devices  129 us
    all_gather x2, blocking collectives, apply_operator(): full_waves = lax.all_gather(incoming, 'near', axis=3, tiled=True)  83.4 us
    ppermute x2, starting transfers between devices, with_halo(): lax.ppermute(lax.slice_in_dim(block, block.shape[dim] - width, None, axis...  9.03 us
    dot_general x2, matrix products, apply_operator(): jnp.einsum('nkrc,nkcd->nrd', both_parts, near_blocks[:, :, 0], preferred_...  8.88 us
    dot_general x2, matrix products, apply_operator(): jnp.einsum('nkrc,nkcd->nrd', both_parts, near_blocks[:, :, 1], preferred_...  8.84 us
    unnamed x20, local copies, waits for them, and re-layouts  7.23 us
    psum x2, blocking collectives, apply_operator(): field = lax.psum(near_field + far_field, 'far')  7.18 us
  transfers between devices with their start and end apart: 6, of which 3 were waited for; matrix products, arithmetic and copies ran while one was open for 11% of the time, Pallas kernels for 0%

commit v1 on v0

--- a/solution.py
+++ b/solution.py
@@ -91,7 +91,25 @@
         picked[:, :, :, 1],
     )
     incoming = jnp.stack([jnp.sum(in_re, axis=1), jnp.sum(in_im, axis=1)], axis=2)
-    full_waves = lax.all_gather(incoming, "near", axis=3, tiled=True)
+    size, index, rows = (lax.axis_size("near"), lax.axis_index("near"), incoming.shape[3])
+    forward_2 = [(i_2, (i_2 + 1) % size) for i_2 in range(size)]
+    behind = [(i_2, (i_2 - 1) % size) for i_2 in range(size)]
+    full_waves = jnp.zeros(
+        (*incoming.shape[:3], size * rows, *incoming.shape[3 + 1 :]), incoming.dtype
+    )
+    full_waves = lax.dynamic_update_slice_in_dim(full_waves, incoming, index * rows, axis=3)
+    from_left = from_right = incoming
+    halfway = size // 2
+    for step in range(1, halfway + 1):
+        from_left = lax.ppermute(from_left, "near", forward_2)
+        full_waves = lax.dynamic_update_slice_in_dim(
+            full_waves, from_left, (index - step) % size * rows, axis=3
+        )
+        if step < size - halfway:
+            from_right = lax.ppermute(from_right, "near", behind)
+            full_waves = lax.dynamic_update_slice_in_dim(
+                full_waves, from_right, (index + step) % size * rows, axis=3
+            )
     owner = (
         sphere_box[:, None] == far_pos * own_boxes + jnp.arange(own_boxes, dtype=jnp.int32)[None, :]
     ).astype(jnp.float32)

time: 291 us -> 359 us (1.23)
  blocking collectives: 94.3 us -> 11.1 us
  starting transfers between devices: 11.7 us -> 89.1 us
  local copies, waits for them, and re-layouts: 12.1 us -> 50.1 us
  waiting for transfers between devices: 130 us -> 166 us
    all_gather x2 -> x0, blocking collectives: 83.4 us -> none  [apply_operator(): full_waves = lax.all_gather(incoming, 'near', axis=3, tiled=True)]
    ppermute x0 -> x30, starting transfers between devices: none -> 80.1 us  [the longest x14 79.9 us: apply_operator(): from_right = lax.ppermute(from_right, 'near', behind)]
    dynamic_update_slice x0 -> x32, local copies, waits for them, and re-layouts: none -> 38 us  [the longest x14 18.9 us: apply_operator(): lax.dynamic_update_slice_in_dim(full_waves, from_right, (index + step) %...]
    unnamed x4, waiting for transfers between devices: 129 us -> 152 us
    ppermute x0 -> x30, waiting for transfers between devices: none -> 14.3 us  [the longest x16 10.9 us: apply_operator(): from_left = lax.ppermute(from_left, 'near', forward_2)]
  transfers between devices with their start and end apart: 6 -> 36, of which waited for: 3 -> 16; matrix products, arithmetic and copies ran while one was open for 11% -> 20% of each run, Pallas kernels for 0% -> 0%
where the time goes in v1:
time: 359 us
  waiting for transfers between devices  166 us (46%)
  starting transfers between devices  89.1 us (25%)
  local copies, waits for them, and re-layouts  50.1 us (14%)
  matrix products  22.7 us (6%)
  between operations  15 us (4%)
  blocking collectives  11.1 us (3%)
  other arithmetic  4.18 us (1%)
    unnamed x4, waiting for transfers between devices  152 us
    ppermute x14, starting transfers between devices, apply_operator(): from_right = lax.ppermute(from_right, 'near', behind)  79.9 us
    dynamic_update_slice x14, local copies, waits for them, and re-layouts, apply_operator(): lax.dynamic_update_slice_in_dim(full_waves, from_right, (index + step) %...  18.9 us
    dynamic_update_slice x16, local copies, waits for them, and re-layouts, apply_operator(): lax.dynamic_update_slice_in_dim(full_waves, from_left, (index - step) % s...  18.5 us
    ppermute x16, waiting for transfers between devices, apply_operator(): from_left = lax.ppermute(from_left, 'near', forward_2)  10.9 us
    dot_general x2, matrix products, apply_operator(): jnp.einsum('nkrc,nkcd->nrd', both_parts, near_blocks[:, :, 1], preferred_...  8.83 us
    dot_general x2, matrix products, apply_operator(): jnp.einsum('nkrc,nkcd->nrd', both_parts, near_blocks[:, :, 0], preferred_...  8.83 us
    psum x2, blocking collectives, apply_operator(): field = lax.psum(near_field + far_field, 'far')  7.36 us
  transfers between devices with their start and end apart: 36, of which 16 were waited for; matrix products, arithmetic and copies ran while one was open for 20% of the time, Pallas kernels for 0%

profile of v1, /device:TPU:0, one launch (start us, length us, event | category | flops | bytes accessed | tf_op | source)
XLA Modules:
  0.0 358.5 jit_solution(302043328521063693)
XLA Ops:
  7.2 5.0 %collective-permute-start = (bf16[8,4,480]{2,1,0:T(4,128)(2,1)}, bf16[8,4,480]{2,1,0:T(4,128)(2,1)S(1)}, u32[]{:S(2)}, u32[]{:S(2)}) collective-permute-start(bf16[8,4,480]{2,1,0:T(4,128)(2,1)} %param.11), channel_id=1, source_target_pairs={{0,2},{2,4},{4,6},{6,8},{8,10},{10,12},{12,14},{14,16},{16,18},{18... | collective-permute-start | bytes 92168 | tf_op jit(solution)/shard_map/ppermute | solution.py:12
  12.3 1.3 collective-permute-start.1
  14.3 1.3 fusion.25
  17.3 1.9 reshape.112
  22.8 76.0 %reduce-scatter.7.cloned.1.call-done = f32[16,64]{1,0:T(8,128)} async-done(((f32[256,64]{1,0:T(8,128)}), f32[16,64]{1,0:T(8,128)}) %reduce-scatter.7.cloned.1.call-update) | async-done | bytes 4112
  99.7 1.8 all_gather.6
  103.0 5.5 %collective-permute-start.3 = (f32[8,4,2,16]{3,1,0,2:T(4,128)S(1)}, f32[8,4,2,16]{3,1,0,2:T(4,128)S(1)}, u32[]{:S(2)}, u32[]{:S(2)}) collective-permute-start(f32[8,4,2,16]{3,1,0,2:T(4,128)S(1)} %pad_maximum_fusion.8), channel_id=1, source_target_pairs={{0,30},{2,0},{4,2},{6,4},{8,6},{10,8},{12,10},{14,12},{16,14},{18,... | collective-permute-start | bytes 12296 | tf_op jit(solution)/shard_map/ppermute | solution.py:109
  108.5 1.9 collective-permute-done.2
  110.4 5.6 %collective-permute-start.5 = (f32[8,4,2,16]{3,1,0,2:T(4,128)S(1)}, f32[8,4,2,16]{3,1,0,2:T(4,128)S(1)}, u32[]{:S(2)}, u32[]{:S(2)}) collective-permute-start(f32[8,4,2,16]{3,1,0,2:T(4,128)S(1)} %collective-permute-done.3), channel_id=1, source_target_pairs={{0,30},{2,0},{4,2},{6,4},{8,6},{10,8},{12,10},{14,12},{16,14},{18,... | collective-permute-start | bytes 12296 | tf_op jit(solution)/shard_map/ppermute | solution.py:109
  116.0 1.9 collective-permute-done.4
  119.6 5.7 %collective-permute-start.7 = (f32[8,4,2,16]{3,1,0,2:T(4,128)S(1)}, f32[8,4,2,16]{3,1,0,2:T(4,128)S(1)}, u32[]{:S(2)}, u32[]{:S(2)}) collective-permute-start(f32[8,4,2,16]{3,1,0,2:T(4,128)S(1)} %collective-permute-done.5), channel_id=1, source_target_pairs={{0,30},{2,0},{4,2},{6,4},{8,6},{10,8},{12,10},{14,12},{16,14},{18,... | collective-permute-start | bytes 12296 | tf_op jit(solution)/shard_map/ppermute | solution.py:109
  126.8 5.9 %collective-permute-start.9 = (f32[8,4,2,16]{3,1,0,2:T(4,128)S(1)}, f32[8,4,2,16]{3,1,0,2:T(4,128)S(1)}, u32[]{:S(2)}, u32[]{:S(2)}) collective-permute-start(f32[8,4,2,16]{3,1,0,2:T(4,128)S(1)} %collective-permute-done.7), channel_id=1, source_target_pairs={{0,30},{2,0},{4,2},{6,4},{8,6},{10,8},{12,10},{14,12},{16,14},{18,... | collective-permute-start | bytes 12296 | tf_op jit(solution)/shard_map/ppermute | solution.py:109
  133.1 1.3 collective-permute-done.9
  134.3 5.9 %collective-permute-start.11 = (f32[8,4,2,16]{3,1,0,2:T(4,128)S(1)}, f32[8,4,2,16]{3,1,0,2:T(4,128)S(1)}, u32[]{:S(2)}, u32[]{:S(2)}) collective-permute-start(f32[8,4,2,16]{3,1,0,2:T(4,128)S(1)} %collective-permute-done.9), channel_id=1, source_target_pairs={{0,30},{2,0},{4,2},{6,4},{8,6},{10,8},{12,10},{14,12},{16,14},{18,... | collective-permute-start | bytes 12296 | tf_op jit(solution)/shard_map/ppermute | solution.py:109
  140.5 4.4 %fusion.12 = f32[8,8,240]{2,1,0:T(8,128)S(1)} fusion(bf16[8,8,2,240,240]{4,3,2,1,0:T(8,128)(2,1)} %param.12, bf16[8,8,4,240]{3,2,1,0:T(4,128)(2,1)S(1)} %get-tuple-element.9, bf16[8,8,4,240]{3,2,1,0:T(4,128)(2,1)S(1)} %get-tuple-element.8), kind=kOutput, calls=%fused_computation.14 | convolution fusion | flops 59473920 | bytes 8171520 | tf_op jit(solution)/shard_map/nkrc,nkcd->nrd/dot_general | solution.py:65
  144.9 5.6 %collective-permute-start.13 = (f32[8,4,2,16]{3,1,0,2:T(4,128)S(1)}, f32[8,4,2,16]{3,1,0,2:T(4,128)S(1)}, u32[]{:S(2)}, u32[]{:S(2)}) collective-permute-start(f32[8,4,2,16]{3,1,0,2:T(4,128)S(1)} %collective-permute-done.11), channel_id=1, source_target_pairs={{0,30},{2,0},{4,2},{6,4},{8,6},{10,8},{12,10},{14,12},{16,14},{18,... | collective-permute-start | bytes 12296 | tf_op jit(solution)/shard_map/ppermute | solution.py:109
  150.5 4.4 %fusion.18 = f32[8,8,240]{2,1,0:T(8,128)S(1)} fusion(bf16[8,8,2,240,240]{4,3,2,1,0:T(8,128)(2,1)} %param.12, bf16[8,8,4,240]{3,2,1,0:T(4,128)(2,1)S(1)} %get-tuple-element.9, bf16[8,8,4,240]{3,2,1,0:T(4,128)(2,1)S(1)} %get-tuple-element.8), kind=kOutput, calls=%fused_computation.16 | convolution fusion | flops 59473920 | bytes 8171520 | tf_op jit(solution)/shard_map/nkrc,nkcd->nrd/dot_general | solution.py:68
  154.9 5.6 %collective-permute-start.15 = (f32[8,4,2,16]{3,1,0,2:T(4,128)S(1)}, f32[8,4,2,16]{3,1,0,2:T(4,128)S(1)}, u32[]{:S(2)}, u32[]{:S(2)}) collective-permute-start(f32[8,4,2,16]{3,1,0,2:T(4,128)S(1)} %collective-permute-done.13), channel_id=1, source_target_pairs={{0,30},{2,0},{4,2},{6,4},{8,6},{10,8},{12,10},{14,12},{16,14},{18,... | collective-permute-start | bytes 12296 | tf_op jit(solution)/shard_map/ppermute | solution.py:109
  161.0 1.3 dynamic_update_slice.97
  162.3 1.4 dynamic_update_slice.98
  163.6 1.3 dynamic_update_slice.99
  164.9 1.4 dynamic_update_slice.100
  166.3 1.3 dynamic_update_slice.101
  167.6 1.4 dynamic_update_slice.102
  169.0 1.3 dynamic_update_slice.103
  170.3 1.4 dynamic_update_slice.104
  171.7 1.3 dynamic_update_slice.105
  173.0 1.4 dynamic_update_slice.106
  174.3 1.3 dynamic_update_slice.107
  175.6 1.4 dynamic_update_slice.108
  177.0 1.3 dynamic_update_slice.109
  178.3 1.4 dynamic_update_slice.110
  180.5 3.8 %psum.14 = f32[8,4,480]{2,1,0:T(4,128)S(1)} all-reduce(f32[8,4,480]{2,1,0:T(4,128)S(1)} %convolution_add_fusion.1), channel_id=1, replica_groups=mesh['near'=16,'far'=2] {'far'}, use_global_device_ids=true, to_apply=%region_3.4 | all-reduce | flops 15360 | bytes 122880 | tf_op jit(solution)/shard_map/psum | solution.py:127
  185.7 1.9 reshape.114
  187.7 1.3 collective-permute-start.17
  189.0 1.3 collective-permute-start.18
  190.3 75.9 %reduce-scatter.9.cloned.1.call-done = f32[16,64]{1,0:T(8,128)} async-done(((f32[256,64]{1,0:T(8,128)}), f32[16,64]{1,0:T(8,128)}) %reduce-scatter.9.cloned.1.call-update) | async-done | bytes 4112
  267.1 1.8 all_gather.7
  269.6 5.6 %collective-permute-start.20 = (f32[8,4,2,16]{3,1,0,2:T(4,128)S(1)}, f32[8,4,2,16]{3,1,0,2:T(4,128)S(1)}, u32[]{:S(2)}, u32[]{:S(2)}) collective-permute-start(f32[8,4,2,16]{3,1,0,2:T(4,128)S(1)} %pad_maximum_fusion.10), channel_id=1, source_target_pairs={{0,30},{2,0},{4,2},{6,4},{8,6},{10,8},{12,10},{14,12},{16,14},{18,... | collective-permute-start | bytes 12296 | tf_op jit(solution)/shard_map/ppermute | solution.py:109
  275.3 1.9 collective-permute-done.19
  277.1 5.6 %collective-permute-start.22 = (f32[8,4,2,16]{3,1,0,2:T(4,128)S(1)}, f32[8,4,2,16]{3,1,0,2:T(4,128)S(1)}, u32[]{:S(2)}, u32[]{:S(2)}) collective-permute-start(f32[8,4,2,16]{3,1,0,2:T(4,128)S(1)} %collective-permute-done.20), channel_id=1, source_target_pairs={{0,30},{2,0},{4,2},{6,4},{8,6},{10,8},{12,10},{14,12},{16,14},{18,... | collective-permute-start | bytes 12296 | tf_op jit(solution)/shard_map/ppermute | solution.py:109
  282.8 1.9 collective-permute-done.21
  285.6 5.7 %collective-permute-start.24 = (f32[8,4,2,16]{3,1,0,2:T(4,128)S(1)}, f32[8,4,2,16]{3,1,0,2:T(4,128)S(1)}, u32[]{:S(2)}, u32[]{:S(2)}) collective-permute-start(f32[8,4,2,16]{3,1,0,2:T(4,128)S(1)} %collective-permute-done.22), channel_id=1, source_target_pairs={{0,30},{2,0},{4,2},{6,4},{8,6},{10,8},{12,10},{14,12},{16,14},{18,... | collective-permute-start | bytes 12296 | tf_op jit(solution)/shard_map/ppermute | solution.py:109
  292.8 5.9 %collective-permute-start.26 = (f32[8,4,2,16]{3,1,0,2:T(4,128)S(1)}, f32[8,4,2,16]{3,1,0,2:T(4,128)S(1)}, u32[]{:S(2)}, u32[]{:S(2)}) collective-permute-start(f32[8,4,2,16]{3,1,0,2:T(4,128)S(1)} %collective-permute-done.24), channel_id=1, source_target_pairs={{0,30},{2,0},{4,2},{6,4},{8,6},{10,8},{12,10},{14,12},{16,14},{18,... | collective-permute-start | bytes 12296 | tf_op jit(solution)/shard_map/ppermute | solution.py:109
  300.4 5.9 %collective-permute-start.28 = (f32[8,4,2,16]{3,1,0,2:T(4,128)S(1)}, f32[8,4,2,16]{3,1,0,2:T(4,128)S(1)}, u32[]{:S(2)}, u32[]{:S(2)}) collective-permute-start(f32[8,4,2,16]{3,1,0,2:T(4,128)S(1)} %collective-permute-done.26), channel_id=1, source_target_pairs={{0,30},{2,0},{4,2},{6,4},{8,6},{10,8},{12,10},{14,12},{16,14},{18,... | collective-permute-start | bytes 12296 | tf_op jit(solution)/shard_map/ppermute | solution.py:109
  307.2 4.4 %fusion.15 = f32[8,8,240]{2,1,0:T(8,128)S(1)} fusion(bf16[8,8,2,240,240]{4,3,2,1,0:T(8,128)(2,1)} %param.12, bf16[8,8,4,240]{3,2,1,0:T(4,128)(2,1)S(1)} %get-tuple-element.7, bf16[8,8,4,240]{3,2,1,0:T(4,128)(2,1)S(1)} %get-tuple-element.6), kind=kOutput, calls=%fused_computation.15 | convolution fusion | flops 59473920 | bytes 8171520 | tf_op jit(solution)/shard_map/nkrc,nkcd->nrd/dot_general | solution.py:65
  311.6 5.6 %collective-permute-start.30 = (f32[8,4,2,16]{3,1,0,2:T(4,128)S(1)}, f32[8,4,2,16]{3,1,0,2:T(4,128)S(1)}, u32[]{:S(2)}, u32[]{:S(2)}) collective-permute-start(f32[8,4,2,16]{3,1,0,2:T(4,128)S(1)} %collective-permute-done.28), channel_id=1, source_target_pairs={{0,30},{2,0},{4,2},{6,4},{8,6},{10,8},{12,10},{14,12},{16,14},{18,... | collective-permute-start | bytes 12296 | tf_op jit(solution)/shard_map/ppermute | solution.py:109
  317.3 4.4 %fusion.21 = f32[8,8,240]{2,1,0:T(8,128)S(1)} fusion(bf16[8,8,2,240,240]{4,3,2,1,0:T(8,128)(2,1)} %param.12, bf16[8,8,4,240]{3,2,1,0:T(4,128)(2,1)S(1)} %get-tuple-element.7, bf16[8,8,4,240]{3,2,1,0:T(4,128)(2,1)S(1)} %get-tuple-element.6), kind=kOutput, calls=%fused_computation.17 | convolution fusion | flops 59473920 | bytes 8171520 | tf_op jit(solution)/shard_map/nkrc,nkcd->nrd/dot_general | solution.py:68
  321.7 5.6 %collective-permute-start.32 = (f32[8,4,2,16]{3,1,0,2:T(4,128)S(1)}, f32[8,4,2,16]{3,1,0,2:T(4,128)S(1)}, u32[]{:S(2)}, u32[]{:S(2)}) collective-permute-start(f32[8,4,2,16]{3,1,0,2:T(4,128)S(1)} %collective-permute-done.30), channel_id=1, source_target_pairs={{0,30},{2,0},{4,2},{6,4},{8,6},{10,8},{12,10},{14,12},{16,14},{18,... | collective-permute-start | bytes 12296 | tf_op jit(solution)/shard_map/ppermute | solution.py:109
  327.7 1.3 dynamic_update_slice.113
  329.0 1.4 dynamic_update_slice.114
  330.4 1.3 dynamic_update_slice.115
  331.7 1.4 dynamic_update_slice.116
  333.0 1.3 dynamic_update_slice.117
  334.4 1.4 dynamic_update_slice.118
  335.7 1.3 dynamic_update_slice.119
  337.0 1.4 dynamic_update_slice.120
  338.4 1.3 dynamic_update_slice.121
  339.7 1.4 dynamic_update_slice.122
  341.1 1.3 dynamic_update_slice.123
  342.4 1.4 dynamic_update_slice.124
  343.8 1.3 dynamic_update_slice.125
  345.1 1.4 dynamic_update_slice.126
  347.3 3.6 %psum.15 = f32[8,4,480]{2,1,0:T(4,128)S(1)} all-reduce(f32[8,4,480]{2,1,0:T(4,128)S(1)} %convolution_add_fusion), channel_id=1, replica_groups=mesh['near'=16,'far'=2] {'far'}, use_global_device_ids=true, to_apply=%region_7.8 | all-reduce | flops 15360 | bytes 122880 | tf_op jit(solution)/shard_map/psum | solution.py:127
  (148 shorter events, 23.2 us)
Async XLA Ops:
  7.2 173.1 %copy-start = (bf16[512,480]{0,1:T(8,128)(2,1)S(1)}, bf16[512,480]{0,1:T(8,128)(2,1)}, u32[]{:S(2)}) copy-start(bf16[512,480]{0,1:T(8,128)(2,1)} %param.21) | copy-start | bytes 1474564
  7.2 172.8 %copy-start.5 = (s32[8]{0:T(128)S(1)}, s32[8]{0:T(128)}, u32[]{:S(2)}) copy-start(s32[8]{0:T(128)} %param.17) | copy-start | bytes 100
  7.2 91.6 %reduce-scatter.7.cloned.1.call-start = ((), (), s32[]{:S(2)}) async-start(), calls=%async_computation.2 | async-start | bytes 139264
  7.2 110.7 %collective-permute-start = (bf16[8,4,480]{2,1,0:T(4,128)(2,1)}, bf16[8,4,480]{2,1,0:T(4,128)(2,1)S(1)}, u32[]{:S(2)}, u32[]{:S(2)}) collective-permute-start(bf16[8,4,480]{2,1,0:T(4,128)(2,1)} %param.11), channel_id=1, source_target_pairs={{0,2},{2,4},{4,6},{6,8},{8,10},{10,12},{12,14},{14,16},{16,18},{18... | collective-permute-start | bytes 92168 | tf_op jit(solution)/shard_map/ppermute | solution.py:12
  12.3 105.7 %collective-permute-start.1 = (bf16[8,4,480]{2,1,0:T(4,128)(2,1)}, bf16[8,4,480]{2,1,0:T(4,128)(2,1)S(1)}, u32[]{:S(2)}, u32[]{:S(2)}) collective-permute-start(bf16[8,4,480]{2,1,0:T(4,128)(2,1)} %param.11), channel_id=1, source_target_pairs={{2,0},{4,2},{6,4},{8,6},{10,8},{12,10},{14,12},{16,14},{18,16},{20... | collective-permute-start | bytes 92168 | tf_op jit(solution)/shard_map/ppermute | solution.py:15
  14.3 170.1 %copy-start.3 = (bf16[8,4,480]{2,1,0:T(4,128)(2,1)S(1)}, bf16[8,4,480]{2,1,0:T(4,128)(2,1)}, u32[]{:S(2)}) copy-start(bf16[8,4,480]{2,1,0:T(4,128)(2,1)} %param.11) | copy-start | bytes 92164
  14.3 170.2 %copy-start.1 = (bf16[480,512]{1,0:T(8,128)(2,1)S(1)}, bf16[480,512]{1,0:T(8,128)(2,1)}, u32[]{:S(2)}) copy-start(bf16[480,512]{1,0:T(8,128)(2,1)} %param.16) | copy-start | bytes 1474564
  19.3 246.9 %reduce-scatter.9.cloned.1.call-start = ((), (), s32[]{:S(2)}) async-start(), calls=%async_computation.3 | async-start | bytes 139264
  22.8 246.2 %copy-start.4 = (s32[8,16]{1,0:T(8,128)S(1)}, s32[8,16]{1,0:T(8,128)}, u32[]{:S(2)}) copy-start(s32[8,16]{1,0:T(8,128)} %param.19) | copy-start | bytes 1540
  102.8 7.6 %collective-permute-start.2 = (f32[8,4,2,16]{3,1,0,2:T(4,128)S(1)}, f32[8,4,2,16]{3,1,0,2:T(4,128)S(1)}, u32[]{:S(2)}, u32[]{:S(2)}) collective-permute-start(f32[8,4,2,16]{3,1,0,2:T(4,128)S(1)} %pad_maximum_fusion.8), channel_id=1, source_target_pairs={{0,2},{2,4},{4,6},{6,8},{8,10},{10,12},{12,14},{14,16},{16,18},{18... | collective-permute-start | bytes 12296 | tf_op jit(solution)/shard_map/ppermute | solution.py:104
  103.0 7.4 %collective-permute-start.3 = (f32[8,4,2,16]{3,1,0,2:T(4,128)S(1)}, f32[8,4,2,16]{3,1,0,2:T(4,128)S(1)}, u32[]{:S(2)}, u32[]{:S(2)}) collective-permute-start(f32[8,4,2,16]{3,1,0,2:T(4,128)S(1)} %pad_maximum_fusion.8), channel_id=1, source_target_pairs={{0,30},{2,0},{4,2},{6,4},{8,6},{10,8},{12,10},{14,12},{16,14},{18,... | collective-permute-start | bytes 12296 | tf_op jit(solution)/shard_map/ppermute | solution.py:109
  110.4 7.5 %collective-permute-start.4 = (f32[8,4,2,16]{3,1,0,2:T(4,128)S(1)}, f32[8,4,2,16]{3,1,0,2:T(4,128)S(1)}, u32[]{:S(2)}, u32[]{:S(2)}) collective-permute-start(f32[8,4,2,16]{3,1,0,2:T(4,128)S(1)} %collective-permute-done.2), channel_id=1, source_target_pairs={{0,2},{2,4},{4,6},{6,8},{8,10},{10,12},{12,14},{14,16},{16,18},{18... | collective-permute-start | bytes 12296 | tf_op jit(solution)/shard_map/ppermute | solution.py:104
  110.4 9.2 %collective-permute-start.5 = (f32[8,4,2,16]{3,1,0,2:T(4,128)S(1)}, f32[8,4,2,16]{3,1,0,2:T(4,128)S(1)}, u32[]{:S(2)}, u32[]{:S(2)}) collective-permute-start(f32[8,4,2,16]{3,1,0,2:T(4,128)S(1)} %collective-permute-done.3), channel_id=1, source_target_pairs={{0,30},{2,0},{4,2},{6,4},{8,6},{10,8},{12,10},{14,12},{16,14},{18,... | collective-permute-start | bytes 12296 | tf_op jit(solution)/shard_map/ppermute | solution.py:109
  117.9 7.5 %collective-permute-start.6 = (f32[8,4,2,16]{3,1,0,2:T(4,128)S(1)}, f32[8,4,2,16]{3,1,0,2:T(4,128)S(1)}, u32[]{:S(2)}, u32[]{:S(2)}) collective-permute-start(f32[8,4,2,16]{3,1,0,2:T(4,128)S(1)} %collective-permute-done.4), channel_id=1, source_target_pairs={{0,2},{2,4},{4,6},{6,8},{8,10},{10,12},{12,14},{14,16},{16,18},{18... | collective-permute-start | bytes 12296 | tf_op jit(solution)/shard_map/ppermute | solution.py:104
  119.6 7.3 %collective-permute-start.7 = (f32[8,4,2,16]{3,1,0,2:T(4,128)S(1)}, f32[8,4,2,16]{3,1,0,2:T(4,128)S(1)}, u32[]{:S(2)}, u32[]{:S(2)}) collective-permute-start(f32[8,4,2,16]{3,1,0,2:T(4,128)S(1)} %collective-permute-done.5), channel_id=1, source_target_pairs={{0,30},{2,0},{4,2},{6,4},{8,6},{10,8},{12,10},{14,12},{16,14},{18,... | collective-permute-start | bytes 12296 | tf_op jit(solution)/shard_map/ppermute | solution.py:109
  125.4 7.5 %collective-permute-start.8 = (f32[8,4,2,16]{3,1,0,2:T(4,128)S(1)}, f32[8,4,2,16]{3,1,0,2:T(4,128)S(1)}, u32[]{:S(2)}, u32[]{:S(2)}) collective-permute-start(f32[8,4,2,16]{3,1,0,2:T(4,128)S(1)} %collective-permute-done.6), channel_id=1, source_target_pairs={{0,2},{2,4},{4,6},{6,8},{8,10},{10,12},{12,14},{14,16},{16,18},{18... | collective-permute-start | bytes 12296 | tf_op jit(solution)/shard_map/ppermute | solution.py:104
  126.8 7.5 %collective-permute-start.9 = (f32[8,4,2,16]{3,1,0,2:T(4,128)S(1)}, f32[8,4,2,16]{3,1,0,2:T(4,128)S(1)}, u32[]{:S(2)}, u32[]{:S(2)}) collective-permute-start(f32[8,4,2,16]{3,1,0,2:T(4,128)S(1)} %collective-permute-done.7), channel_id=1, source_target_pairs={{0,30},{2,0},{4,2},{6,4},{8,6},{10,8},{12,10},{14,12},{16,14},{18,... | collective-permute-start | bytes 12296 | tf_op jit(solution)/shard_map/ppermute | solution.py:109
  132.9 7.5 %collective-permute-start.10 = (f32[8,4,2,16]{3,1,0,2:T(4,128)S(1)}, f32[8,4,2,16]{3,1,0,2:T(4,128)S(1)}, u32[]{:S(2)}, u32[]{:S(2)}) collective-permute-start(f32[8,4,2,16]{3,1,0,2:T(4,128)S(1)} %collective-permute-done.8), channel_id=1, source_target_pairs={{0,2},{2,4},{4,6},{6,8},{8,10},{10,12},{12,14},{14,16},{16,18},{18... | collective-permute-start | bytes 12296 | tf_op jit(solution)/shard_map/ppermute | solution.py:104
  134.3 10.5 %collective-permute-start.11 = (f32[8,4,2,16]{3,1,0,2:T(4,128)S(1)}, f32[8,4,2,16]{3,1,0,2:T(4,128)S(1)}, u32[]{:S(2)}, u32[]{:S(2)}) collective-permute-start(f32[8,4,2,16]{3,1,0,2:T(4,128)S(1)} %collective-permute-done.9), channel_id=1, source_target_pairs={{0,30},{2,0},{4,2},{6,4},{8,6},{10,8},{12,10},{14,12},{16,14},{18,... | collective-permute-start | bytes 12296 | tf_op jit(solution)/shard_map/ppermute | solution.py:109
  140.5 10.1 %collective-permute-start.12 = (f32[8,4,2,16]{3,1,0,2:T(4,128)S(1)}, f32[8,4,2,16]{3,1,0,2:T(4,128)S(1)}, u32[]{:S(2)}, u32[]{:S(2)}) collective-permute-start(f32[8,4,2,16]{3,1,0,2:T(4,128)S(1)} %collective-permute-done.10), channel_id=1, source_target_pairs={{0,2},{2,4},{4,6},{6,8},{8,10},{10,12},{12,14},{14,16},{16,18},{18... | collective-permute-start | bytes 12296 | tf_op jit(solution)/shard_map/ppermute | solution.py:104
  144.9 10.1 %collective-permute-start.13 = (f32[8,4,2,16]{3,1,0,2:T(4,128)S(1)}, f32[8,4,2,16]{3,1,0,2:T(4,128)S(1)}, u32[]{:S(2)}, u32[]{:S(2)}) collective-permute-start(f32[8,4,2,16]{3,1,0,2:T(4,128)S(1)} %collective-permute-done.11), channel_id=1, source_target_pairs={{0,30},{2,0},{4,2},{6,4},{8,6},{10,8},{12,10},{14,12},{16,14},{18,... | collective-permute-start | bytes 12296 | tf_op jit(solution)/shard_map/ppermute | solution.py:109
  150.5 10.1 %collective-permute-start.14 = (f32[8,4,2,16]{3,1,0,2:T(4,128)S(1)}, f32[8,4,2,16]{3,1,0,2:T(4,128)S(1)}, u32[]{:S(2)}, u32[]{:S(2)}) collective-permute-start(f32[8,4,2,16]{3,1,0,2:T(4,128)S(1)} %collective-permute-done.12), channel_id=1, source_target_pairs={{0,2},{2,4},{4,6},{6,8},{8,10},{10,12},{12,14},{14,16},{16,18},{18... | collective-permute-start | bytes 12296 | tf_op jit(solution)/shard_map/ppermute | solution.py:104
  154.9 23.4 %collective-permute-start.15 = (f32[8,4,2,16]{3,1,0,2:T(4,128)S(1)}, f32[8,4,2,16]{3,1,0,2:T(4,128)S(1)}, u32[]{:S(2)}, u32[]{:S(2)}) collective-permute-start(f32[8,4,2,16]{3,1,0,2:T(4,128)S(1)} %collective-permute-done.13), channel_id=1, source_target_pairs={{0,30},{2,0},{4,2},{6,4},{8,6},{10,8},{12,10},{14,12},{16,14},{18,... | collective-permute-start | bytes 12296 | tf_op jit(solution)/shard_map/ppermute | solution.py:109
  160.6 19.1 %collective-permute-start.16 = (f32[8,4,2,16]{3,1,0,2:T(4,128)S(1)}, f32[8,4,2,16]{3,1,0,2:T(4,128)S(1)}, u32[]{:S(2)}, u32[]{:S(2)}) collective-permute-start(f32[8,4,2,16]{3,1,0,2:T(4,128)S(1)} %collective-permute-done.14), channel_id=1, source_target_pairs={{0,2},{2,4},{4,6},{6,8},{8,10},{10,12},{12,14},{14,16},{16,18},{18... | collective-permute-start | bytes 12296 | tf_op jit(solution)/shard_map/ppermute | solution.py:104
  184.5 167.1 %copy-start.2 = (bf16[8,4,480]{2,1,0:T(4,128)(2,1)}, bf16[8,4,480]{2,1,0:T(4,128)(2,1)S(1)}, u32[]{:S(2)}) copy-start(bf16[8,4,480]{2,1,0:T(4,128)(2,1)S(1)} %fusion.34) | copy-start | bytes 92164
  187.7 97.0 %collective-permute-start.17 = (bf16[8,4,480]{2,1,0:T(4,128)(2,1)S(1)}, bf16[8,4,480]{2,1,0:T(4,128)(2,1)S(1)}, u32[]{:S(2)}, u32[]{:S(2)}) collective-permute-start(bf16[8,4,480]{2,1,0:T(4,128)(2,1)S(1)} %fusion.34), channel_id=1, source_target_pairs={{0,2},{2,4},{4,6},{6,8},{8,10},{10,12},{12,14},{14,16},{16,18},{18... | collective-permute-start | bytes 92168 | tf_op jit(solution)/shard_map/ppermute | solution.py:12
  189.0 95.7 %collective-permute-start.18 = (bf16[8,4,480]{2,1,0:T(4,128)(2,1)S(1)}, bf16[8,4,480]{2,1,0:T(4,128)(2,1)S(1)}, u32[]{:S(2)}, u32[]{:S(2)}) collective-permute-start(bf16[8,4,480]{2,1,0:T(4,128)(2,1)S(1)} %fusion.34), channel_id=1, source_target_pairs={{2,0},{4,2},{6,4},{8,6},{10,8},{12,10},{14,12},{16,14},{18,16},{20... | collective-permute-start | bytes 92168 | tf_op jit(solution)/shard_map/ppermute | solution.py:15
  269.6 7.6 %collective-permute-start.19 = (f32[8,4,2,16]{3,1,0,2:T(4,128)S(1)}, f32[8,4,2,16]{3,1,0,2:T(4,128)S(1)}, u32[]{:S(2)}, u32[]{:S(2)}) collective-permute-start(f32[8,4,2,16]{3,1,0,2:T(4,128)S(1)} %pad_maximum_fusion.10), channel_id=1, source_target_pairs={{0,2},{2,4},{4,6},{6,8},{8,10},{10,12},{12,14},{14,16},{16,18},{18... | collective-permute-start | bytes 12296 | tf_op jit(solution)/shard_map/ppermute | solution.py:104
  269.6 7.5 %collective-permute-start.20 = (f32[8,4,2,16]{3,1,0,2:T(4,128)S(1)}, f32[8,4,2,16]{3,1,0,2:T(4,128)S(1)}, u32[]{:S(2)}, u32[]{:S(2)}) collective-permute-start(f32[8,4,2,16]{3,1,0,2:T(4,128)S(1)} %pad_maximum_fusion.10), channel_id=1, source_target_pairs={{0,30},{2,0},{4,2},{6,4},{8,6},{10,8},{12,10},{14,12},{16,14},{18,... | collective-permute-start | bytes 12296 | tf_op jit(solution)/shard_map/ppermute | solution.py:109
  277.1 7.5 %collective-permute-start.21 = (f32[8,4,2,16]{3,1,0,2:T(4,128)S(1)}, f32[8,4,2,16]{3,1,0,2:T(4,128)S(1)}, u32[]{:S(2)}, u32[]{:S(2)}) collective-permute-start(f32[8,4,2,16]{3,1,0,2:T(4,128)S(1)} %collective-permute-done.19), channel_id=1, source_target_pairs={{0,2},{2,4},{4,6},{6,8},{8,10},{10,12},{12,14},{14,16},{16,18},{18... | collective-permute-start | bytes 12296 | tf_op jit(solution)/shard_map/ppermute | solution.py:104
  277.1 8.4 %collective-permute-start.22 = (f32[8,4,2,16]{3,1,0,2:T(4,128)S(1)}, f32[8,4,2,16]{3,1,0,2:T(4,128)S(1)}, u32[]{:S(2)}, u32[]{:S(2)}) collective-permute-start(f32[8,4,2,16]{3,1,0,2:T(4,128)S(1)} %collective-permute-done.20), channel_id=1, source_target_pairs={{0,30},{2,0},{4,2},{6,4},{8,6},{10,8},{12,10},{14,12},{16,14},{18,... | collective-permute-start | bytes 12296 | tf_op jit(solution)/shard_map/ppermute | solution.py:109
  284.7 7.5 %collective-permute-start.23 = (f32[8,4,2,16]{3,1,0,2:T(4,128)S(1)}, f32[8,4,2,16]{3,1,0,2:T(4,128)S(1)}, u32[]{:S(2)}, u32[]{:S(2)}) collective-permute-start(f32[8,4,2,16]{3,1,0,2:T(4,128)S(1)} %collective-permute-done.21), channel_id=1, source_target_pairs={{0,2},{2,4},{4,6},{6,8},{8,10},{10,12},{12,14},{14,16},{16,18},{18... | collective-permute-start | bytes 12296 | tf_op jit(solution)/shard_map/ppermute | solution.py:104
  285.6 7.3 %collective-permute-start.24 = (f32[8,4,2,16]{3,1,0,2:T(4,128)S(1)}, f32[8,4,2,16]{3,1,0,2:T(4,128)S(1)}, u32[]{:S(2)}, u32[]{:S(2)}) collective-permute-start(f32[8,4,2,16]{3,1,0,2:T(4,128)S(1)} %collective-permute-done.22), channel_id=1, source_target_pairs={{0,30},{2,0},{4,2},{6,4},{8,6},{10,8},{12,10},{14,12},{16,14},{18,... | collective-permute-start | bytes 12296 | tf_op jit(solution)/shard_map/ppermute | solution.py:109
  292.2 7.5 %collective-permute-start.25 = (f32[8,4,2,16]{3,1,0,2:T(4,128)S(1)}, f32[8,4,2,16]{3,1,0,2:T(4,128)S(1)}, u32[]{:S(2)}, u32[]{:S(2)}) collective-permute-start(f32[8,4,2,16]{3,1,0,2:T(4,128)S(1)} %collective-permute-done.23), channel_id=1, source_target_pairs={{0,2},{2,4},{4,6},{6,8},{8,10},{10,12},{12,14},{14,16},{16,18},{18... | collective-permute-start | bytes 12296 | tf_op jit(solution)/shard_map/ppermute | solution.py:104
  292.8 7.5 %collective-permute-start.26 = (f32[8,4,2,16]{3,1,0,2:T(4,128)S(1)}, f32[8,4,2,16]{3,1,0,2:T(4,128)S(1)}, u32[]{:S(2)}, u32[]{:S(2)}) collective-permute-start(f32[8,4,2,16]{3,1,0,2:T(4,128)S(1)} %collective-permute-done.24), channel_id=1, source_target_pairs={{0,30},{2,0},{4,2},{6,4},{8,6},{10,8},{12,10},{14,12},{16,14},{18,... | collective-permute-start | bytes 12296 | tf_op jit(solution)/shard_map/ppermute | solution.py:109
  299.7 7.5 %collective-permute-start.27 = (f32[8,4,2,16]{3,1,0,2:T(4,128)S(1)}, f32[8,4,2,16]{3,1,0,2:T(4,128)S(1)}, u32[]{:S(2)}, u32[]{:S(2)}) collective-permute-start(f32[8,4,2,16]{3,1,0,2:T(4,128)S(1)} %collective-permute-done.25), channel_id=1, source_target_pairs={{0,2},{2,4},{4,6},{6,8},{8,10},{10,12},{12,14},{14,16},{16,18},{18... | collective-permute-start | bytes 12296 | tf_op jit(solution)/shard_map/ppermute | solution.py:104
  300.4 11.3 %collective-permute-start.28 = (f32[8,4,2,16]{3,1,0,2:T(4,128)S(1)}, f32[8,4,2,16]{3,1,0,2:T(4,128)S(1)}, u32[]{:S(2)}, u32[]{:S(2)}) collective-permute-start(f32[8,4,2,16]{3,1,0,2:T(4,128)S(1)} %collective-permute-done.26), channel_id=1, source_target_pairs={{0,30},{2,0},{4,2},{6,4},{8,6},{10,8},{12,10},{14,12},{16,14},{18,... | collective-permute-start | bytes 12296 | tf_op jit(solution)/shard_map/ppermute | solution.py:109
  307.2 10.1 %collective-permute-start.29 = (f32[8,4,2,16]{3,1,0,2:T(4,128)S(1)}, f32[8,4,2,16]{3,1,0,2:T(4,128)S(1)}, u32[]{:S(2)}, u32[]{:S(2)}) collective-permute-start(f32[8,4,2,16]{3,1,0,2:T(4,128)S(1)} %collective-permute-done.27), channel_id=1, source_target_pairs={{0,2},{2,4},{4,6},{6,8},{8,10},{10,12},{12,14},{14,16},{16,18},{18... | collective-permute-start | bytes 12296 | tf_op jit(solution)/shard_map/ppermute | solution.py:104
  311.6 10.1 %collective-permute-start.30 = (f32[8,4,2,16]{3,1,0,2:T(4,128)S(1)}, f32[8,4,2,16]{3,1,0,2:T(4,128)S(1)}, u32[]{:S(2)}, u32[]{:S(2)}) collective-permute-start(f32[8,4,2,16]{3,1,0,2:T(4,128)S(1)} %collective-permute-done.28), channel_id=1, source_target_pairs={{0,30},{2,0},{4,2},{6,4},{8,6},{10,8},{12,10},{14,12},{16,14},{18,... | collective-permute-start | bytes 12296 | tf_op jit(solution)/shard_map/ppermute | solution.py:109
  317.3 10.1 %collective-permute-start.31 = (f32[8,4,2,16]{3,1,0,2:T(4,128)S(1)}, f32[8,4,2,16]{3,1,0,2:T(4,128)S(1)}, u32[]{:S(2)}, u32[]{:S(2)}) collective-permute-start(f32[8,4,2,16]{3,1,0,2:T(4,128)S(1)} %collective-permute-done.29), channel_id=1, source_target_pairs={{0,2},{2,4},{4,6},{6,8},{8,10},{10,12},{12,14},{14,16},{16,18},{18... | collective-permute-start | bytes 12296 | tf_op jit(solution)/shard_map/ppermute | solution.py:104
  321.7 23.4 %collective-permute-start.32 = (f32[8,4,2,16]{3,1,0,2:T(4,128)S(1)}, f32[8,4,2,16]{3,1,0,2:T(4,128)S(1)}, u32[]{:S(2)}, u32[]{:S(2)}) collective-permute-start(f32[8,4,2,16]{3,1,0,2:T(4,128)S(1)} %collective-permute-done.30), channel_id=1, source_target_pairs={{0,30},{2,0},{4,2},{6,4},{8,6},{10,8},{12,10},{14,12},{16,14},{18,... | collective-permute-start | bytes 12296 | tf_op jit(solution)/shard_map/ppermute | solution.py:109
  327.3 19.1 %collective-permute-start.33 = (f32[8,4,2,16]{3,1,0,2:T(4,128)S(1)}, f32[8,4,2,16]{3,1,0,2:T(4,128)S(1)}, u32[]{:S(2)}, u32[]{:S(2)}) collective-permute-start(f32[8,4,2,16]{3,1,0,2:T(4,128)S(1)} %collective-permute-done.31), channel_id=1, source_target_pairs={{0,2},{2,4},{4,6},{6,8},{8,10},{10,12},{12,14},{14,16},{16,18},{18... | collective-permute-start | bytes 12296 | tf_op jit(solution)/shard_map/ppermute | solution.py:104
Sparse Core Ops, SparseCore 0:
  19.4 79.3 reduce-scatter.6
  187.8 78.3 reduce-scatter.8
